TPU v7x, 512 devices: a whole 4x8x8 slice. The times are simulated.
512 devices in a mesh: px: 32 (over y, x), qy: 16 (over z, core).
Axes of the slice: x: 4, y: 8, z: 8, core: 2. Of those that a mesh axis runs over, the one named last changes fastest.
Arguments:
- rhs: float32 [16, 512, 8192], P(None, 'px', 'qy'), may hold values from -9 to 9
- iterate: float32 [16, 512, 8192], P(None, 'px', 'qy'), may hold values from -1.2 to 1.2
- diff_price: float32 [512, 8192], P('px', 'qy'), may hold values from 0.05 to 1
- diff_inventory: float32 [512, 8192], P('px', 'qy'), may hold values from 0.05 to 1
- drift: float32 [512, 8192], P('px', 'qy'), may hold values from 0.05 to 0.5
- boundary: int32 [512, 8192], P('px', 'qy'), may hold values 0 or 1
- drift_sign: int32 [512, 8192], P('px', 'qy'), may hold values 0 or 1
Outputs:
- solution: float32 [16, 512, 8192], P(None, 'px', 'qy')
- residual: float32 [16, 512, 8192], P(None, 'px', 'qy')
All inputs are finite; a program needn't handle non-finite values. No bound on the sum of `boundary` or of `drift_sign` on one device may be relied on, other than what follows from the above.
Results may differ from a plain program's by a relative error of at most 0.0035.
Values sent between devices are 32-bit elements; how exact they have to be, the bound alone decides.
A program may use at most 64 MiB of HBM per device.

v0:
```python
import jax
import jax.numpy as jnp
from jax import lax
from jax.experimental import pallas as pl
from jax.experimental.pallas import tpu as pltpu
from jax.sharding import PartitionSpec as P

STEPS = 4
CYCLES = 2
SIGMA = 5.5
THETA = 4.5
HALO = STEPS
NR = 16
ROWS = 16
COLS = 512
TILES = COLS // 128
WIDE = COLS + 128
EXT = ROWS + 2 * HALO
BASIS = NR * (STEPS + 1)
MESH = pl.DeviceIdType.MESH
F32 = jnp.float32
BF16 = jnp.bfloat16
AROUND = [(a, b) for a in (-1, 0, 1) for b in (-1, 0, 1) if (a, b) != (0, 0)]


def limbs(x):
    high = x.astype(BF16)
    rest = x - high.astype(F32)
    mid = rest.astype(BF16)
    low = (rest - mid.astype(F32)).astype(BF16)
    return high, mid, low


def pick_edges(right, left):
    lane = lax.broadcasted_iota(jnp.int32, right.shape, right.ndim - 1)
    return jnp.where(lane < 64, right, left)


def kernel(
    npx, nqy,
    rhs_hbm, x_hbm, dp_hbm, di_hbm, dr_hbm, bd_hbm, sg_hbm,
    sol_hbm, res_hbm,
    rhs_v, x_in, dp_v, di_v, dr_v, bd_v, sg_v,
    cx, cl, cr, xx, xl, xr,
    p0, hl, hr, pk, basis,
    rs_out, rs_buf, gs_buf, ag_buf, packed_v,
    in_sem, c_send, c_recv, x_send, x_recv, h_send, h_recv,
    sum_send, sum_recv,
):
    px, qy = lax.axis_index("px"), lax.axis_index("qy")

    loads = []
    pairs = [(dp_hbm, dp_v), (di_hbm, di_v), (dr_hbm, dr_v), (bd_hbm, bd_v), (sg_hbm, sg_v)]
    for src, dst in ((x_hbm, x_in), (rhs_hbm, rhs_v)):
        for c in range(TILES):
            pairs.append((src.at[:, pl.ds(c * 128, 128)], dst.at[c]))
    for n, (src, dst) in enumerate(pairs):
        load = pltpu.make_async_copy(src, dst, in_sem.at[n])
        load.start()
        loads.append(load)

    cx[...] = jnp.zeros_like(cx)
    cl[...] = jnp.zeros_like(cl)
    cr[...] = jnp.zeros_like(cr)
    for edge in (0, ROWS + 1):
        xx[edge] = jnp.zeros((NR, WIDE), F32)
    xl[...] = jnp.zeros_like(xl)
    xr[...] = jnp.zeros_like(xr)
    hl[...] = jnp.zeros_like(hl)
    hr[...] = jnp.zeros_like(hr)
    for t in range(CYCLES):
        p0[t, pl.ds(0, HALO)] = jnp.zeros((HALO, NR, WIDE), F32)
        p0[t, pl.ds(HALO + ROWS, HALO)] = jnp.zeros((HALO, NR, WIDE), F32)

    def inside(a, b):
        return (px + a >= 0) & (px + a < npx) & (qy + b >= 0) & (qy + b < nqy)

    def device(a, b):
        return {"px": px + a, "qy": qy + b}

    barrier = pltpu.get_barrier_semaphore()

    @pl.loop(1, nqy)
    def _(s):
        pl.semaphore_signal(
            barrier, inc=1, device_id={"px": px, "qy": lax.rem(qy + s, nqy)}, device_id_type=MESH
        )

    @pl.loop(1, npx)
    def _(s):
        pl.semaphore_signal(
            barrier, inc=1, device_id={"px": lax.rem(px + s, npx), "qy": qy}, device_id_type=MESH
        )

    count = nqy - 1 + npx - 1
    for a in (-1, 1):
        for b in (-1, 1):
            count += inside(a, b).astype(jnp.int32)

            @pl.when(inside(a, b))
            def _():
                pl.semaphore_signal(barrier, inc=1, device_id=device(a, b), device_id_type=MESH)

    for load in loads[: 5 + TILES]:
        load.wait()
    active = (1 - bd_v[...]).astype(F32)
    upward = sg_v[...].astype(F32)
    own = pl.ds(8, ROWS)
    cx[1, own, pl.ds(0, COLS)] = active * dp_v[...]
    cx[2, own, pl.ds(0, COLS)] = active * (di_v[...] + dr_v[...] * upward)
    cx[3, own, pl.ds(0, COLS)] = active * (di_v[...] + dr_v[...] * (1.0 - upward))

    @pl.loop(0, ROWS)
    def _(i):
        for c in range(TILES):
            xx[1 + i, :, pl.ds(c * 128, 128)] = x_in[c, pl.ds(i, NR, stride=ROWS), :]

    pl.semaphore_wait(barrier, count)

    def exchange(copies):
        for (a, b), copy in copies:
            pl.when(inside(a, b))(copy.start)

    def arrive(copies):
        for (a, b), copy in copies:
            pl.when(inside(-a, -b))(copy.wait_recv)

    def left_device(copies):
        for (a, b), copy in copies:
            pl.when(inside(a, b))(copy.wait_send)

    def remote(src, dst, send, recv, a, b):
        return pltpu.make_async_remote_copy(
            src_ref=src, dst_ref=dst, send_sem=send, recv_sem=recv,
            device_id=device(a, b), device_id_type=MESH,
        )

    field_copies, x_copies = [], []
    three = pl.ds(1, 3)
    for n, (a, b) in enumerate(AROUND):
        from_rows = {-1: pl.ds(8, 8), 0: own, 1: pl.ds(16, 8)}[a]
        to_rows = {-1: pl.ds(24, 8), 0: own, 1: pl.ds(0, 8)}[a]
        from_cols = {-1: pl.ds(0, 128), 0: pl.ds(0, COLS), 1: pl.ds(COLS - 128, 128)}[b]
        src = cx.at[three, from_rows, from_cols]
        if b == 0:
            dst = cx.at[three, to_rows, from_cols]
        else:
            dst = (cr if b < 0 else cl).at[three, to_rows]
        field_copies.append(((a, b), remote(src, dst, c_send.at[n], c_recv.at[n], a, b)))
        if a != 0 and b != 0:
            continue
        if b == 0:
            src = xx.at[1 if a < 0 else ROWS, :, from_cols]
            dst = xx.at[ROWS + 1 if a < 0 else 0, :, from_cols]
        else:
            src = xx.at[pl.ds(1, ROWS), :, from_cols]
            dst = xr if b < 0 else xl
        x_copies.append(((a, b), remote(src, dst, x_send.at[n], x_recv.at[n], a, b)))
    exchange(x_copies)
    exchange(field_copies)

    def rim_copies(t):
        copies = []
        for n, (a, b) in enumerate(AROUND):
            from_rows = {-1: pl.ds(HALO, HALO), 0: pl.ds(HALO, ROWS), 1: pl.ds(ROWS, HALO)}[a]
            to_rows = {-1: pl.ds(HALO + ROWS, HALO), 0: pl.ds(HALO, ROWS), 1: pl.ds(0, HALO)}[a]
            from_cols = {-1: pl.ds(0, 128), 0: pl.ds(0, COLS), 1: pl.ds(COLS - 128, 128)}[b]
            src = p0.at[t, from_rows, :, from_cols]
            if b == 0:
                dst = p0.at[t, to_rows, :, from_cols]
            else:
                dst = (hr if b < 0 else hl).at[t, to_rows]
            copies.append(((a, b), remote(src, dst, h_send.at[t, n], h_recv.at[t, n], a, b)))
        return copies

    def image_row(above, center, below, row):
        def field(n):
            return cx[n, pl.ds(row, 1), :]

        return (
            field(0) * center
            - field(1) * (above + below)
            - field(2) * pltpu.roll(center, 1, 1)
            - field(3) * pltpu.roll(center, WIDE - 1, 1)
        )

    for load in loads[5 + TILES :]:
        load.wait()
    arrive(x_copies)
    arrive(field_copies)
    for n in (1, 2, 3):
        cx[n, :, pl.ds(COLS, 128)] = pick_edges(cr[n], cl[n])
    cx[0] = 1.0 + 2.0 * cx[1] + cx[2] + cx[3]

    @pl.loop(0, ROWS)
    def _(i):
        xx[1 + i, :, pl.ds(COLS, 128)] = pick_edges(xr[i], xl[i])
        value = image_row(xx[i], xx[1 + i], xx[2 + i], 8 + i)
        for c in range(TILES):
            p0[0, HALO + i, :, pl.ds(c * 128, 128)] = (
                rhs_v[c, pl.ds(i, NR, stride=ROWS), :] - value[:, c * 128 : c * 128 + 128]
            )

    left_device(x_copies)
    left_device(field_copies)

    def keep_limbs(i, block, value):
        for n, limb in enumerate(limbs(value)):
            basis[i, pl.ds(n * BASIS + block * NR, NR), :] = limb

    def total(t, local):
        for j in range(nqy):
            rs_out[j] = local[2 * j : 2 * j + 2]
        rs_buf[t, qy] = rs_out[qy]

        def scatter(s):
            there = lax.rem(qy + s, nqy)
            return pltpu.make_async_remote_copy(
                src_ref=rs_out.at[there], dst_ref=rs_buf.at[t, qy],
                send_sem=sum_send.at[0], recv_sem=sum_recv.at[t, 0],
                device_id={"px": px, "qy": there}, device_id_type=MESH,
            )

        def along_px(s):
            there = lax.rem(px + s, npx)
            return pltpu.make_async_remote_copy(
                src_ref=gs_buf.at[t, px], dst_ref=gs_buf.at[t, px],
                send_sem=sum_send.at[1], recv_sem=sum_recv.at[t, 1],
                device_id={"px": there, "qy": qy}, device_id_type=MESH,
            )

        def along_qy(s):
            there = lax.rem(qy + s, nqy)
            return pltpu.make_async_remote_copy(
                src_ref=ag_buf.at[t, qy], dst_ref=ag_buf.at[t, qy],
                send_sem=sum_send.at[2], recv_sem=sum_recv.at[t, 2],
                device_id={"px": px, "qy": there}, device_id_type=MESH,
            )

        def run(copy, size, buf, phase):
            @pl.loop(1, size)
            def _(s):
                copy(s).start()

            whole = pltpu.make_async_remote_copy(
                src_ref=buf.at[t, pl.ds(0, size - 1)], dst_ref=buf.at[t, pl.ds(0, size - 1)],
                send_sem=sum_send.at[phase], recv_sem=sum_recv.at[t, phase],
                device_id={"px": px, "qy": qy}, device_id_type=MESH,
            )
            whole.wait_recv()
            whole.wait_send()

        run(scatter, nqy, rs_buf, 0)
        gs_buf[t, px] = jnp.sum(rs_buf[t], axis=0)
        run(along_px, npx, gs_buf, 1)
        ag_buf[t, qy] = jnp.sum(gs_buf[t], axis=0)
        run(along_qy, nqy, ag_buf, 2)
        for j in range(nqy):
            packed_v[pl.ds(2 * j, 2), :] = ag_buf[t, j]
        return packed_v[...]

    def solve(both):
        at = lax.broadcasted_iota(jnp.int32, both.shape, 0)
        for n in range(NR * STEPS):
            row = both[n : n + 1, :]
            row = row / both[n : n + 1, n : n + 1]
            both = jnp.where(at == n, row, both - both[:, n : n + 1] * row)
        return both

    for t in range(CYCLES):
        last = t == CYCLES - 1
        rims = rim_copies(t)
        exchange(rims)

        @pl.loop(0, ROWS)
        def _(i):
            keep_limbs(i, STEPS, p0[t, HALO + i, :, pl.ds(0, COLS)])

        arrive(rims)

        @pl.loop(0, EXT)
        def _(i):
            p0[t, i, :, pl.ds(COLS, 128)] = pick_edges(hr[t, i], hl[t, i])

        for k in range(STEPS):
            src = p0.at[t] if k == 0 else pk.at[k - 1]

            def image_at(i, src=src):
                center = src[i]
                return image_row(src[i - 1], center, src[i + 1], 8 - HALO + i), center

            if k < STEPS - 1:
                for begin, end in ((k + 1, HALO), (HALO + ROWS, EXT - k - 1)):
                    @pl.loop(begin, end)
                    def _(i):
                        image, center = image_at(i)
                        pk[k, i] = image * (1.0 / THETA) - center * (SIGMA / THETA)

            @pl.loop(HALO, HALO + ROWS)
            def _(i):
                image, center = image_at(i)
                if k < STEPS - 1:
                    pk[k, i] = image * (1.0 / THETA) - center * (SIGMA / THETA)
                keep_limbs(i - HALO, k, image[:, :COLS])

        def gram_step(i, acc):
            part = basis[i]
            return acc + lax.dot_general(
                part, part, (((1,), (1,)), ((), ())), preferred_element_type=F32
            )

        acc = lax.fori_loop(0, ROWS, gram_step, jnp.zeros((3 * BASIS, 3 * BASIS), F32))
        rows = acc[2 * BASIS :] + acc[BASIS : 2 * BASIS] + acc[:BASIS]
        gram = rows[:64, 2 * BASIS :] + rows[:64, BASIS : 2 * BASIS] + rows[:64, :BASIS]
        gram = jnp.concatenate([gram, jnp.zeros((64, 48), F32)], axis=1)
        lane = lax.broadcasted_iota(jnp.int32, (32, 128), 1)
        packed = jnp.where(lane < 80, gram[:32], pltpu.roll(gram[32:], 48, 1))
        packed = total(t, packed)
        lower = pltpu.roll(packed, 80, 1)
        square = jnp.concatenate([packed, jnp.zeros((96, 128), F32)], axis=0)
        turned = square.T
        lower = jnp.where(lane < 32, turned[32:64], lower)
        answer = solve(jnp.concatenate([packed, lower], axis=0))
        left_device(rims)

        u = [answer[NR * k : NR * (k + 1)] for k in range(STEPS)]
        e = [None] * STEPS
        e[STEPS - 1] = u[STEPS - 1]
        for k in range(STEPS - 2, -1, -1):
            e[k] = u[k] - (SIGMA / THETA) * e[k + 1]
        lane = lax.broadcasted_iota(jnp.int32, (NR, 128), 1)
        blocks = []
        for k in range(STEPS + 1):
            to_res = -u[k] if k < STEPS else jnp.zeros_like(u[0])
            if k == STEPS:
                to_sol = e[0]
            elif k < STEPS - 1:
                to_sol = e[k + 1] * (1.0 / THETA)
            else:
                to_sol = jnp.zeros_like(u[0])
            blocks.append(jnp.where(lane < 80, to_res, pltpu.roll(to_sol, NR, 1)))
        blocks.append(jnp.zeros((48, 128), F32))
        weights = jnp.concatenate(blocks, axis=0).T[64:96, :BASIS]
        high, mid, low = limbs(weights)
        two = jnp.concatenate([high, mid], axis=0)
        three_limbs = jnp.concatenate([high, mid, low], axis=0)

        @pl.loop(0, ROWS)
        def _(i):
            def product(w, n):
                return jnp.dot(
                    w, basis[i, pl.ds(n * BASIS, BASIS), :], preferred_element_type=F32
                )

            d, f, g = product(three_limbs, 0), product(two, 1), product(high, 2)
            change = ((d[64:] + f[32:] + g) + (d[32:64] + f[:32])) + d[:32]
            res = p0[t, HALO + i, :, pl.ds(0, COLS)] + change[:NR]
            sol = xx[1 + i, :, pl.ds(0, COLS)] + change[NR:]
            if last:
                for c in range(TILES):
                    rhs_v[c, pl.ds(i, NR, stride=ROWS), :] = res[:, c * 128 : c * 128 + 128]
                    x_in[c, pl.ds(i, NR, stride=ROWS), :] = sol[:, c * 128 : c * 128 + 128]
            else:
                p0[t + 1, HALO + i, :, pl.ds(0, COLS)] = res
                xx[1 + i, :, pl.ds(0, COLS)] = sol

    stores = []
    for src, dst in ((x_in, sol_hbm), (rhs_v, res_hbm)):
        for c in range(TILES):
            store = pltpu.make_async_copy(
                src.at[c], dst.at[:, pl.ds(c * 128, 128)], in_sem.at[len(stores)]
            )
            store.start()
            stores.append(store)
    for store in stores:
        store.wait()


def solution(mesh):
    npx, nqy = mesh.shape["px"], mesh.shape["qy"]

    def per_device(rhs, iterate, *fields):
        flat = jax.ShapeDtypeStruct((NR * ROWS, COLS), F32)
        vmem = pltpu.VMEM
        dma = pltpu.SemaphoreType.DMA
        sol, res = pl.pallas_call(
            lambda *refs: kernel(npx, nqy, *refs),
            out_shape=(flat, flat),
            in_specs=[pl.BlockSpec(memory_space=pl.ANY)] * 7,
            out_specs=(pl.BlockSpec(memory_space=pl.ANY),) * 2,
            scratch_shapes=[
                vmem((TILES, NR * ROWS, 128), F32),
                vmem((TILES, NR * ROWS, 128), F32),
                vmem((ROWS, COLS), F32),
                vmem((ROWS, COLS), F32),
                vmem((ROWS, COLS), F32),
                vmem((ROWS, COLS), jnp.int32),
                vmem((ROWS, COLS), jnp.int32),
                vmem((4, ROWS + 16, WIDE), F32),
                vmem((4, ROWS + 16, 128), F32),
                vmem((4, ROWS + 16, 128), F32),
                vmem((ROWS + 2, NR, WIDE), F32),
                vmem((ROWS, NR, 128), F32),
                vmem((ROWS, NR, 128), F32),
                vmem((CYCLES, EXT, NR, WIDE), F32),
                vmem((CYCLES, EXT, NR, 128), F32),
                vmem((CYCLES, EXT, NR, 128), F32),
                vmem((STEPS - 1, EXT, NR, WIDE), F32),
                vmem((ROWS, 3 * BASIS, COLS), BF16),
                vmem((nqy, 2, 128), F32),
                vmem((CYCLES, nqy, 2, 128), F32),
                vmem((CYCLES, npx, 2, 128), F32),
                vmem((CYCLES, nqy, 2, 128), F32),
                vmem((2 * nqy, 128), F32),
                dma((5 + 2 * TILES,)),
                dma((8,)), dma((8,)), dma((8,)), dma((8,)),
                dma((CYCLES, 8)), dma((CYCLES, 8)),
                dma((3,)), dma((CYCLES, 3)),
            ],
            compiler_params=pltpu.CompilerParams(
                collective_id=0, has_side_effects=True, vmem_limit_bytes=48 * 1024 * 1024
            ),
        )(rhs.reshape(NR * ROWS, COLS), iterate.reshape(NR * ROWS, COLS), *fields)
        return sol.reshape(NR, ROWS, COLS), res.reshape(NR, ROWS, COLS)

    whole, plane = P(None, "px", "qy"), P("px", "qy")
    return jax.shard_map(
        per_device, mesh=mesh, in_specs=(whole, whole) + (plane,) * 5,
        out_specs=(whole, whole), check_vma=False,
    )
```

profile of v0, /device:TPU:1, one launch (start us, length us, event | category | flops | bytes accessed | tf_op | source)
XLA Modules:
  0.0 118.4 jit_solution(9776065218282386328)
XLA Ops:
  0.6 0.0 copy-start
  0.6 1.0 copy-done
  1.7 0.0 copy-start.1
  1.7 1.0 copy-done.1
  2.7 0.0 copy-start.2
  2.7 0.8 copy-done.2
  3.5 0.0 copy-start.3
  3.5 0.8 copy-done.3
  4.2 0.0 copy-start.4
  4.2 0.8 copy-done.4
  5.0 0.0 copy-start.5
  5.0 0.8 copy-done.5
  5.8 0.0 copy-start.6
  5.8 0.8 copy-done.6
  6.5 110.3 %shard_map.86 = (f32[256,512]{1,0:T(8,128)S(1)}, f32[256,512]{1,0:T(8,128)S(1)}) custom-call(f32[256,512]{1,0:T(8,128)S(1)} %bitcast.4, f32[256,512]{1,0:T(8,128)S(1)} %bitcast.5, f32[16,512]{1,0:T(8,128)S(1)} %copy-done.2, f32[16,512]{1,0:T(8,128)S(1)} %copy-done.3, f32[16,512]{1,0:T(8,128)S(1)} %copy-done.4, s32[16,512]{1,0:T(8,128)S(1)} %copy-done.5, ...), custom_call_target="tpu_custom_call" | custom-call | tf_op jit(solution)/shard_map/pallas_call | solution.py:386
  116.8 0.8 copy.11
  117.6 0.8 copy.12
Async XLA Ops:
  0.6 1.0 copy-start
  1.7 1.0 copy-start.1
  2.7 0.8 copy-start.2
  3.5 0.8 copy-start.3
  4.2 0.8 copy-start.4
  5.0 0.8 copy-start.5
  5.8 0.8 copy-start.6
where the time goes:
time: 119 us; the launch traced here: 118 us
  Pallas kernels  110 us (92%)
  local copies, waits for them, and re-layouts  7.45 us (6%)
    pallas_call x1, Pallas kernels, per_device(): pl.pallas_call(lambda *refs: kernel(npx, nqy, *refs), out_shape=(flat, fl...  110 us
    unnamed x16, local copies, waits for them, and re-layouts  7.45 us

commit v1 on v0

v1 whole, which is shorter than its diff:
```python
import jax
import jax.numpy as jnp
from jax import lax
from jax.experimental import pallas as pl
from jax.experimental.pallas import tpu as pltpu
from jax.sharding import PartitionSpec as P

STEPS = 4
CYCLES = 2
SIGMA = 5.5
THETA = 4.5
HALO = STEPS
NR = 16
ROWS = 16
COLS = 512
TILES = COLS // 128
WIDE = COLS + 128
EXT = ROWS + 2 * HALO
BASIS = NR * (STEPS + 1)
CORES = 2
CHIPS_X = 4
MESH = pl.DeviceIdType.MESH
F32 = jnp.float32
BF16 = jnp.bfloat16
AROUND = [(a, b) for a in (-1, 0, 1) for b in (-1, 0, 1) if (a, b) != (0, 0)]


def limbs(x):
    high = x.astype(BF16)
    rest = x - high.astype(F32)
    mid = rest.astype(BF16)
    low = (rest - mid.astype(F32)).astype(BF16)
    return high, mid, low


def lanes_of(x):
    return lax.broadcasted_iota(jnp.int32, x.shape, x.ndim - 1)


def edge_pair(first, last):
    return jnp.where(lanes_of(first) < 64, first, last)


def pack(pairs):
    packed = jnp.zeros_like(pairs[0])
    lane = lanes_of(packed)
    for n, pair in enumerate(pairs):
        packed = jnp.where(lane // 8 == n, pltpu.roll(pair, (8 * n + 4) % 128, 1), packed)
    return packed


def unpack(packed, n):
    return pltpu.roll(packed, (124 - 8 * n) % 128, 1)


def kernel(
    npx, nqy,
    rhs_hbm, x_hbm, dp_hbm, di_hbm, dr_hbm, bd_hbm, sg_hbm,
    sol_hbm, res_hbm,
    rhs_v, x_in, dp_v, di_v, dr_v, bd_v, sg_v,
    cx, ce, xx, p0, p1, p2, p3, basis,
    x_out, x_side, f_out, f_side, h_out, h_side,
    rs_out, rs_buf, as_buf, ac_buf, ag_buf, packed_v,
    in_sem, c_send, c_recv, x_send, x_recv, h_send, h_recv,
    sum_send, sum_recv,
):
    px, qy = lax.axis_index("px"), lax.axis_index("qy")
    y, x = px // CHIPS_X, px % CHIPS_X
    z, core = qy // CORES, qy % CORES
    ny, nz, nxc = npx // CHIPS_X, nqy // CORES, CHIPS_X * CORES
    xc = x * CORES + core

    def along_z(s):
        there = lax.rem(z + s, nz)
        return there, {"px": px, "qy": there * CORES + core}

    def along_y(s):
        there = lax.rem(y + s, ny)
        return there, {"px": there * CHIPS_X + x, "qy": qy}

    def along_xc(s):
        there = lax.rem(xc + s, nxc)
        return there, {"px": y * CHIPS_X + there // CORES, "qy": z * CORES + there % CORES}

    loads = []
    pairs = [(x_hbm.at[:, pl.ds(c * 128, 128)], x_in.at[c]) for c in range(TILES)]
    pairs += [(dp_hbm, dp_v), (di_hbm, di_v), (dr_hbm, dr_v), (bd_hbm, bd_v), (sg_hbm, sg_v)]
    pairs += [(rhs_hbm.at[:, pl.ds(c * 128, 128)], rhs_v.at[c]) for c in range(TILES)]
    for n, (src, dst) in enumerate(pairs):
        load = pltpu.make_async_copy(src, dst, in_sem.at[n])
        load.start()
        loads.append(load)

    for edge in (0, 24):
        cx[:, pl.ds(edge, 8), :] = jnp.zeros((3, 8, COLS), F32)
    for edge in (0, ROWS + 1):
        xx[edge] = jnp.zeros((2, 8, WIDE), F32)
    for side in (x_side, f_side, h_side):
        side[...] = jnp.zeros_like(side)
    for t in range(CYCLES):
        for edge in (0, HALO + ROWS):
            p0[t, pl.ds(edge, HALO), :, :, pl.ds(0, COLS)] = jnp.zeros((HALO, 2, 8, COLS), F32)

    def inside(a, b):
        return (px + a >= 0) & (px + a < npx) & (qy + b >= 0) & (qy + b < nqy)

    def device(a, b):
        return {"px": px + a, "qy": qy + b}

    barrier = pltpu.get_barrier_semaphore()
    count = jnp.int32(nz + ny + nxc - 3)
    for a, b in AROUND:
        count += inside(a, b).astype(jnp.int32)

        @pl.when(inside(a, b))
        def _():
            pl.semaphore_signal(barrier, inc=1, device_id=device(a, b), device_id_type=MESH)

    for along, size in ((along_z, nz), (along_y, ny), (along_xc, nxc)):
        @pl.loop(1, size)
        def _(s):
            pl.semaphore_signal(barrier, inc=1, device_id=along(s)[1], device_id_type=MESH)

    def start(copies):
        for (a, b), copy in copies:
            pl.when(inside(a, b))(copy.start)

    def arrive(copies):
        for (a, b), copy in copies:
            pl.when(inside(-a, -b))(copy.wait_recv)

    def leave(copies):
        for (a, b), copy in copies:
            pl.when(inside(a, b))(copy.wait_send)

    def remote(src, dst, send, recv, a, b):
        return (a, b), pltpu.make_async_remote_copy(
            src_ref=src, dst_ref=dst, send_sem=send, recv_sem=recv,
            device_id=device(a, b), device_id_type=MESH,
        )

    def edge_copies(out, side, send, recv, corners=True):
        beside, corner = [], []
        for n, (a, b) in enumerate(AROUND):
            if b == 0:
                continue
            s = 0 if b > 0 else 1
            if a == 0:
                beside.append(
                    remote(out, side.at[s, pl.ds(1, 2)], send.at[n], recv.at[n], a, b)
                )
            elif corners:
                from_tile, to_tile = (0, 3) if a < 0 else (1, 0)
                corner.append(
                    remote(out.at[from_tile], side.at[s, to_tile], send.at[n], recv.at[n], a, b)
                )
        return beside, corner

    def both_sides(side, tile):
        lane = lax.broadcasted_iota(jnp.int32, (8, 128), 1)
        return jnp.where(lane % 8 < 4, side[0, tile], side[1, tile])

    for load in loads[:TILES]:
        load.wait()

    def turn(i):
        for c in range(TILES):
            xx[1 + i, :, :, pl.ds(c * 128, 128)] = (
                x_in[c, pl.ds(i, NR, stride=ROWS), :].reshape(2, 8, 128)
            )

    @pl.loop(0, ROWS, unroll=4)
    def _(i):
        turn(i)

    def pack_rows(ref, first, out):
        for tile in range(2):
            pairs = []
            for i in range(8):
                for h in range(2):
                    row = first + 8 * tile + i
                    pairs.append(
                        edge_pair(ref[row, h, :, pl.ds(0, 128)], ref[row, h, :, pl.ds(COLS - 128, 128)])
                    )
            out[tile] = pack(pairs)

    pack_rows(xx, 1, x_out)
    pl.semaphore_wait(barrier, count)
    x_rows = []
    for a in (-1, 1):
        n = AROUND.index((a, 0))
        x_rows.append(remote(
            xx.at[1 if a < 0 else ROWS, :, :, pl.ds(0, COLS)],
            xx.at[ROWS + 1 if a < 0 else 0, :, :, pl.ds(0, COLS)],
            x_send.at[n], x_recv.at[n], a, 0,
        ))
    x_beside, _ = edge_copies(x_out, x_side, x_send, x_recv, corners=False)
    start(x_beside)
    start(x_rows)

    for load in loads[TILES : TILES + 5]:
        load.wait()
    active = (1 - bd_v[...]).astype(F32)
    upward = sg_v[...].astype(F32)
    price = active * dp_v[...]
    lower = active * (di_v[...] + dr_v[...] * upward)
    higher = active * (di_v[...] + dr_v[...] * (1.0 - upward))
    own = pl.ds(8, ROWS)
    for n, field in enumerate((price, lower, higher)):
        cx[n, own, :] = field
    for tile in range(2):
        rows8 = slice(8 * tile, 8 * tile + 8)
        f_out[tile] = pack([
            edge_pair(field[rows8, :128], field[rows8, COLS - 128 :])
            for field in (price, lower, higher)
        ])
    f_rows = []
    for a in (-1, 1):
        n = AROUND.index((a, 0))
        f_rows.append(remote(
            cx.at[:, pl.ds(8 if a < 0 else 16, 8), :], cx.at[:, pl.ds(24 if a < 0 else 0, 8), :],
            c_send.at[n], c_recv.at[n], a, 0,
        ))
    f_beside, f_corner = edge_copies(f_out, f_side, c_send, c_recv)
    f_copies = f_beside + f_rows + f_corner
    start(f_copies)

    def spread(n, row, value, at, width):
        ce[n, row, :, pl.ds(at, width)] = jnp.broadcast_to(value, (8, width))

    diagonal = 1.0 + 2.0 * price + lower + higher
    for n, field in enumerate((diagonal, price, lower, higher)):
        for i in range(ROWS):
            spread(n, HALO + i, field[i : i + 1], 0, COLS)

    def image_row(above, center, below, row, width):
        def field(n):
            return ce[n, row, :, pl.ds(0, width)][None]

        def cut(value):
            return value[:, :, :width]

        return (
            field(0) * cut(center)
            - field(1) * (cut(above) + cut(below))
            - field(2) * cut(pltpu.roll(center, 1, 2))
            - field(3) * cut(pltpu.roll(center, WIDE - 1, 2))
        )

    for load in loads[TILES + 5 :]:
        load.wait()
    arrive(x_beside)
    for i in range(ROWS):
        tile = both_sides(x_side, 1 + i // 8)
        for h in range(2):
            xx[1 + i, h, :, pl.ds(COLS, 128)] = unpack(tile, 2 * (i % 8) + h)
    arrive(x_rows)

    def first_residual(i):
        value = image_row(xx[i], xx[1 + i], xx[2 + i], HALO + i, COLS)
        for c in range(TILES):
            p0[0, HALO + i, :, :, pl.ds(c * 128, 128)] = (
                rhs_v[c, pl.ds(i, NR, stride=ROWS), :].reshape(2, 8, 128)
                - value[:, :, c * 128 : c * 128 + 128]
            )

    def rim_rows(t):
        copies = []
        for a in (-1, 1):
            n = AROUND.index((a, 0))
            copies.append(remote(
                p0.at[t, pl.ds(HALO if a < 0 else ROWS, HALO), :, :, pl.ds(0, COLS)],
                p0.at[t, pl.ds(HALO + ROWS if a < 0 else 0, HALO), :, :, pl.ds(0, COLS)],
                h_send.at[t, n], h_recv.at[t, n], a, 0,
            ))
        return copies

    def outer_rows_first(body, t):
        for begin in (0, ROWS - HALO):
            @pl.loop(begin, begin + HALO, unroll=4)
            def _(i):
                body(i)
        if t < CYCLES:
            start(rim_rows(t))

        @pl.loop(HALO, ROWS - HALO, unroll=4)
        def _(i):
            body(i)

    outer_rows_first(first_residual, 0)

    def total(t, local):
        for j in range(nxc):
            rs_out[j] = local[4 * j : 4 * j + 4]
        rs_buf[t, xc] = rs_out[xc]

        def phase(n, along, size, src, buf, me):
            steps = [s for d in range(size // 2, 0, -1) for s in sorted({d, size - d})]
            for s in steps:
                there, where = along(s)
                pltpu.make_async_remote_copy(
                    src_ref=src(there), dst_ref=buf.at[t, me],
                    send_sem=sum_send.at[n], recv_sem=sum_recv.at[t, n],
                    device_id=where, device_id_type=MESH,
                ).start()
            whole = pltpu.make_async_remote_copy(
                src_ref=buf.at[t, pl.ds(0, size - 1)], dst_ref=buf.at[t, pl.ds(0, size - 1)],
                send_sem=sum_send.at[n], recv_sem=sum_recv.at[t, n],
                device_id={"px": px, "qy": qy}, device_id_type=MESH,
            )
            whole.wait_recv()
            return whole

        sent = [phase(0, along_xc, nxc, lambda there: rs_out.at[there], rs_buf, xc)]
        as_buf[t, y] = jnp.sum(rs_buf[t], axis=0)
        sent.append(phase(1, along_y, ny, lambda there: as_buf.at[t, y], as_buf, y))
        ac_buf[t, z] = jnp.sum(as_buf[t], axis=0)
        sent.append(phase(2, along_z, nz, lambda there: ac_buf.at[t, z], ac_buf, z))
        ag_buf[t, xc] = jnp.sum(ac_buf[t], axis=0)
        sent.append(phase(3, along_xc, nxc, lambda there: ag_buf.at[t, xc], ag_buf, xc))
        for j in range(nxc):
            packed_v[pl.ds(4 * j, 4), :] = ag_buf[t, j]
        return packed_v[...], sent

    def solve(both):
        at = lax.broadcasted_iota(jnp.int32, both.shape, 0)
        for n in range(NR * STEPS):
            row = both[n : n + 1, :]
            row = row / both[n : n + 1, n : n + 1]
            both = jnp.where(at == n, row, both - both[:, n : n + 1] * row)
        return both

    def keep_limbs(i, block, value):
        for n, limb in enumerate(limbs(value[:, :, :COLS].reshape(NR, COLS))):
            basis[i, pl.ds(n * BASIS + block * NR, NR), :] = limb

    for t in range(CYCLES):
        last = t == CYCLES - 1
        fields = [p0.at[t], p1, p2, p3]
        rims = rim_rows(t)
        pack_rows(p0.at[t], HALO, h_out.at[t])
        beside, corner = edge_copies(h_out.at[t], h_side.at[t], h_send.at[t], h_recv.at[t])
        start(beside)
        start(corner)

        @pl.loop(0, ROWS, unroll=4)
        def _(i):
            keep_limbs(i, STEPS, p0[t, HALO + i])

        if t == 0:
            arrive(f_copies)
            for p in range(EXT):
                row = 8 - HALO + p
                tile = both_sides(f_side, row // 8)
                values = [unpack(tile, n)[row % 8 : row % 8 + 1] for n in range(3)]
                values = [1.0 + 2.0 * values[0] + values[1] + values[2]] + values
                for n, value in enumerate(values):
                    spread(n, p, value, COLS, 128)
                if HALO <= p < HALO + ROWS:
                    continue
                values = [cx[n, pl.ds(row, 1), :] for n in range(3)]
                values = [1.0 + 2.0 * values[0] + values[1] + values[2]] + values
                for n, value in enumerate(values):
                    spread(n, p, value, 0, COLS)

        def lanes_around(p):
            row = 8 - HALO + p
            tile = both_sides(h_side.at[t], row // 8)
            for h in range(2):
                p0[t, p, h, :, pl.ds(COLS, 128)] = unpack(tile, 2 * (row % 8) + h)

        def advance(k, rows, inner):
            images = [
                image_row(
                    fields[k][p - 1], fields[k][p], fields[k][p + 1], p,
                    WIDE if k < STEPS - 1 else COLS,
                )
                for p in rows
            ]
            for p, image, own_row in zip(rows, images, inner):
                if k < STEPS - 1:
                    fields[k + 1][p] = image * (1.0 / THETA) - fields[k][p] * (SIGMA / THETA)
                if own_row:
                    keep_limbs(p - HALO, k, image)

        arrive(beside)
        for p in range(HALO, HALO + ROWS):
            lanes_around(p)
        for k in range(STEPS):
            @pl.loop(0, (EXT - 10 - 2 * k) // 2)
            def _(i):
                p = HALO + 1 + k + 2 * i
                advance(k, [p, p + 1], [True, True])

        arrive(rims)
        arrive(corner)
        for begin in (0, HALO + ROWS):
            for p in range(begin, begin + HALO):
                lanes_around(p)
        for k in range(STEPS):
            for begin in (k + 1, EXT - 5 - k):
                rows = [begin + n for n in range(4)]
                inner = [HALO <= p < HALO + ROWS for p in rows]
                if k == STEPS - 1:
                    advance(k, rows, inner)
                else:
                    advance(k, rows[:2], inner[:2])
                    advance(k, rows[2:], inner[2:])

        def gram_step(i, acc):
            for n in range(4):
                part = basis[4 * i + n]
                acc = acc + lax.dot_general(
                    part, part, (((1,), (1,)), ((), ())), preferred_element_type=F32
                )
            return acc

        acc = lax.fori_loop(0, ROWS // 4, gram_step, jnp.zeros((3 * BASIS, 3 * BASIS), F32))
        rows = acc[2 * BASIS :] + acc[BASIS : 2 * BASIS] + acc[:BASIS]
        gram = rows[:64, 2 * BASIS :] + rows[:64, BASIS : 2 * BASIS] + rows[:64, :BASIS]
        gram = jnp.concatenate([gram, jnp.zeros((64, 48), F32)], axis=1)
        lane = lax.broadcasted_iota(jnp.int32, (32, 128), 1)
        packed = jnp.where(lane < 80, gram[:32], pltpu.roll(gram[32:], 48, 1))
        packed, sent = total(t, packed)
        lower = pltpu.roll(packed, 80, 1)
        square = jnp.concatenate([packed, jnp.zeros((96, 128), F32)], axis=0)
        turned = square.T
        lower = jnp.where(lane < 32, turned[32:64], lower)
        answer = solve(jnp.concatenate([packed, lower], axis=0))
        if t == 0:
            leave(x_beside + x_rows + f_copies)
        leave(rims + beside + corner)
        for whole in sent:
            whole.wait_send()

        u = [answer[NR * k : NR * (k + 1)] for k in range(STEPS)]
        e = [None] * STEPS
        e[STEPS - 1] = u[STEPS - 1]
        for k in range(STEPS - 2, -1, -1):
            e[k] = u[k] - (SIGMA / THETA) * e[k + 1]
        lane = lax.broadcasted_iota(jnp.int32, (NR, 128), 1)
        blocks = []
        for k in range(STEPS + 1):
            to_res = -u[k] if k < STEPS else jnp.zeros_like(u[0])
            if k == STEPS:
                to_sol = e[0]
            elif k < STEPS - 1:
                to_sol = e[k + 1] * (1.0 / THETA)
            else:
                to_sol = jnp.zeros_like(u[0])
            blocks.append(jnp.where(lane < 80, to_res, pltpu.roll(to_sol, NR, 1)))
        blocks.append(jnp.zeros((48, 128), F32))
        weights = jnp.concatenate(blocks, axis=0).T[64:96, :BASIS]
        high, mid, low = limbs(weights)
        two = jnp.concatenate([high, mid], axis=0)
        three = jnp.concatenate([high, mid, low], axis=0)

        def update(i):
            def product(w, n):
                return jnp.dot(
                    w, basis[i, pl.ds(n * BASIS, BASIS), :], preferred_element_type=F32
                )

            d, f, g = product(three, 0), product(two, 1), product(high, 2)
            change = ((d[64:] + f[32:] + g) + (d[32:64] + f[:32])) + d[:32]
            res = p0[t, HALO + i, :, :, pl.ds(0, COLS)] + change[:NR].reshape(2, 8, COLS)
            sol = xx[1 + i, :, :, pl.ds(0, COLS)] + change[NR:].reshape(2, 8, COLS)
            if last:
                for c in range(TILES):
                    part = slice(c * 128, c * 128 + 128)
                    rhs_v[c, pl.ds(i, NR, stride=ROWS), :] = res[:, :, part].reshape(NR, 128)
                    x_in[c, pl.ds(i, NR, stride=ROWS), :] = sol[:, :, part].reshape(NR, 128)
            else:
                p0[t + 1, HALO + i, :, :, pl.ds(0, COLS)] = res
                xx[1 + i, :, :, pl.ds(0, COLS)] = sol

        outer_rows_first(update, t + 1)

    stores = []
    for src, dst in ((x_in, sol_hbm), (rhs_v, res_hbm)):
        for c in range(TILES):
            store = pltpu.make_async_copy(
                src.at[c], dst.at[:, pl.ds(c * 128, 128)], in_sem.at[len(stores)]
            )
            store.start()
            stores.append(store)
    for store in stores:
        store.wait()


def solution(mesh):
    npx, nqy = mesh.shape["px"], mesh.shape["qy"]

    def per_device(rhs, iterate, *fields):
        flat = jax.ShapeDtypeStruct((NR * ROWS, COLS), F32)
        vmem = pltpu.VMEM
        dma = pltpu.SemaphoreType.DMA
        field = vmem((EXT, 2, 8, WIDE), F32)
        plane = vmem((ROWS, COLS), F32)
        marks = vmem((ROWS, COLS), jnp.int32)
        turned = vmem((TILES, NR * ROWS, 128), F32)
        eighth = vmem((CYCLES, 8, 4, 128), F32)
        sol, res = pl.pallas_call(
            lambda *refs: kernel(npx, nqy, *refs),
            out_shape=(flat, flat),
            in_specs=[pl.BlockSpec(memory_space=pl.ANY)] * 7,
            out_specs=(pl.BlockSpec(memory_space=pl.ANY),) * 2,
            scratch_shapes=[
                turned, turned, plane, plane, plane, marks, marks,
                vmem((3, ROWS + 16, COLS), F32),
                vmem((4, EXT, 8, WIDE), F32),
                vmem((ROWS + 2, 2, 8, WIDE), F32),
                vmem((CYCLES, EXT, 2, 8, WIDE), F32),
                field, field, field,
                vmem((ROWS, 3 * BASIS, COLS), BF16),
                vmem((2, 8, 128), F32), vmem((2, 4, 8, 128), F32),
                vmem((2, 8, 128), F32), vmem((2, 4, 8, 128), F32),
                vmem((CYCLES, 2, 8, 128), F32), vmem((CYCLES, 2, 4, 8, 128), F32),
                vmem((8, 4, 128), F32), eighth, eighth, eighth, eighth,
                vmem((32, 128), F32),
                dma((5 + 2 * TILES,)),
                dma((8,)), dma((8,)), dma((8,)), dma((8,)),
                dma((CYCLES, 8)), dma((CYCLES, 8)),
                dma((4,)), dma((CYCLES, 4)),
            ],
            compiler_params=pltpu.CompilerParams(
                collective_id=0, has_side_effects=True, vmem_limit_bytes=62 * 1024 * 1024
            ),
        )(rhs.reshape(NR * ROWS, COLS), iterate.reshape(NR * ROWS, COLS), *fields)
        return sol.reshape(NR, ROWS, COLS), res.reshape(NR, ROWS, COLS)

    whole, plane = P(None, "px", "qy"), P("px", "qy")
    return jax.shard_map(
        per_device, mesh=mesh, in_specs=(whole, whole) + (plane,) * 5,
        out_specs=(whole, whole), check_vma=False,
    )
```

time: 119 us -> 88.2 us (0.74)
  Pallas kernels: 110 us -> 84.6 us
  local copies, waits for them, and re-layouts: 7.45 us -> 2.74 us
    pallas_call x1, Pallas kernels: 110 us -> 84.6 us  [per_device(): pl.pallas_call(lambda *refs: kernel(npx, nqy, *refs), out_shape=(flat, fl...]
    unnamed x16 -> x4, local copies, waits for them, and re-layouts: 7.45 us -> 2.74 us
where the time goes in v1:
time: 88.2 us; the launch traced here: 88 us
  Pallas kernels  84.6 us (96%)
  local copies, waits for them, and re-layouts  2.74 us (3%)
    pallas_call x1, Pallas kernels, per_device(): pl.pallas_call(lambda *refs: kernel(npx, nqy, *refs), out_shape=(flat, fl...  84.6 us
    unnamed x4, local copies, waits for them, and re-layouts  2.74 us

profile of v1, /device:TPU:1, one launch (start us, length us, event | category | flops | bytes accessed | tf_op | source)
XLA Modules:
  0.0 88.0 jit_solution(5568704922127710702)
XLA Ops:
  0.6 84.6 %shard_map.86 = (f32[256,512]{1,0:T(8,128)}, f32[256,512]{1,0:T(8,128)}) custom-call(f32[256,512]{1,0:T(8,128)} %bitcast.4, f32[256,512]{1,0:T(8,128)} %bitcast.5, f32[16,512]{1,0:T(8,128)} %refs_2_.1, f32[16,512]{1,0:T(8,128)} %refs_3_.1, f32[16,512]{1,0:T(8,128)} %refs_4_.1, s32[16,512]{1,0:T(8,128)} %refs_5_.1, s32[16,512]{1,0:T(8,128)} %refs_6_.1), custom_call_target="tpu_custom_call" | custom-call | tf_op jit(solution)/shard_map/pallas_call | solution.py:503
  85.3 0.0 copy-start
  85.3 1.9 %copy.11 = f32[16,16,512]{2,1,0:T(8,128)} copy(f32[16,16,512]{2,1,0:T(8,128)} %bitcast.7) | data formatting | bytes 1048576
  87.2 0.0 copy-done
  87.2 0.8 copy.12
Async XLA Ops:
  85.3 2.0 %copy-start = (f32[256,512]{1,0:T(8,128)S(1)}, f32[256,512]{1,0:T(8,128)}, u32[]{:S(2)}) copy-start(f32[256,512]{1,0:T(8,128)} %get-tuple-element.5) | copy-start | bytes 1572868

commit v2 on v1

--- a/solution.py
+++ b/solution.py
@@ -323,12 +323,31 @@
         return packed_v[...], sent
 
     def solve(both):
-        at = lax.broadcasted_iota(jnp.int32, both.shape, 0)
-        for n in range(NR * STEPS):
-            row = both[n : n + 1, :]
-            row = row / both[n : n + 1, n : n + 1]
-            both = jnp.where(at == n, row, both - both[:, n : n + 1] * row)
-        return both
+        tiles = [both[8 * r : 8 * r + 8] for r in range(8)]
+        at = lax.broadcasted_iota(jnp.int32, (8, 128), 0)
+
+        def across(row):
+            return jnp.broadcast_to(row, (8, 128))
+
+        for b in range(8):
+            columns = [
+                [jnp.broadcast_to(tile[:, n : n + 1], (8, 128)) for tile in tiles]
+                for n in range(8 * b, 8 * b + 8)
+            ]
+            for j in range(8):
+                pivots = columns[j]
+                inverse = 1.0 / across(pivots[b][j : j + 1])
+
+                def eliminate(group):
+                    row = across(group[b][j : j + 1]) * inverse
+                    after = [g - c * row for g, c in zip(group, pivots)]
+                    after[b] = jnp.where(at == j, row, after[b])
+                    return after
+
+                for q in range(j + 1, 8):
+                    columns[q] = eliminate(columns[q])
+                tiles = eliminate(tiles)
+        return jnp.concatenate(tiles, axis=0)
 
     def keep_limbs(i, block, value):
         for n, limb in enumerate(limbs(value[:, :, :COLS].reshape(NR, COLS))):
@@ -392,6 +411,16 @@
                 p = HALO + 1 + k + 2 * i
                 advance(k, [p, p + 1], [True, True])
 
+        def gram_step(i, acc):
+            for n in range(4):
+                part = basis[4 * i + n]
+                acc = acc + lax.dot_general(
+                    part, part, (((1,), (1,)), ((), ())), preferred_element_type=F32
+                )
+            return acc
+
+        acc = lax.fori_loop(1, 3, gram_step, jnp.zeros((3 * BASIS, 3 * BASIS), F32))
+
         arrive(rims)
         arrive(corner)
         for begin in (0, HALO + ROWS):
@@ -407,15 +436,7 @@
                     advance(k, rows[:2], inner[:2])
                     advance(k, rows[2:], inner[2:])
 
-        def gram_step(i, acc):
-            for n in range(4):
-                part = basis[4 * i + n]
-                acc = acc + lax.dot_general(
-                    part, part, (((1,), (1,)), ((), ())), preferred_element_type=F32
-                )
-            return acc
-
-        acc = lax.fori_loop(0, ROWS // 4, gram_step, jnp.zeros((3 * BASIS, 3 * BASIS), F32))
+        acc = gram_step(3, gram_step(0, acc))
         rows = acc[2 * BASIS :] + acc[BASIS : 2 * BASIS] + acc[:BASIS]
         gram = rows[:64, 2 * BASIS :] + rows[:64, BASIS : 2 * BASIS] + rows[:64, :BASIS]
         gram = jnp.concatenate([gram, jnp.zeros((64, 48), F32)], axis=1)

time: 88.2 us -> 80.5 us (0.913)
  Pallas kernels: 84.6 us -> 77 us
    pallas_call x1, Pallas kernels: 84.6 us -> 77 us  [per_device(): pl.pallas_call(lambda *refs: kernel(npx, nqy, *refs), out_shape=(flat, fl...]
where the time goes in v2:
time: 80.5 us; the launch traced here: 80.4 us
  Pallas kernels  77 us (96%)
  local copies, waits for them, and re-layouts  2.74 us (3%)
    pallas_call x1, Pallas kernels, per_device(): pl.pallas_call(lambda *refs: kernel(npx, nqy, *refs), out_shape=(flat, fl...  77 us
    unnamed x4, local copies, waits for them, and re-layouts  2.74 us

profile of v2, /device:TPU:1, one launch (start us, length us, event | category | flops | bytes accessed | tf_op | source)
XLA Modules:
  0.0 80.4 jit_solution(5391675145165233673)
XLA Ops:
  0.6 77.0 %shard_map.86 = (f32[256,512]{1,0:T(8,128)}, f32[256,512]{1,0:T(8,128)}) custom-call(f32[256,512]{1,0:T(8,128)} %bitcast.4, f32[256,512]{1,0:T(8,128)} %bitcast.5, f32[16,512]{1,0:T(8,128)} %refs_2_.1, f32[16,512]{1,0:T(8,128)} %refs_3_.1, f32[16,512]{1,0:T(8,128)} %refs_4_.1, s32[16,512]{1,0:T(8,128)} %refs_5_.1, s32[16,512]{1,0:T(8,128)} %refs_6_.1), custom_call_target="tpu_custom_call" | custom-call | tf_op jit(solution)/shard_map/pallas_call | solution.py:524
  77.6 0.0 copy-start
  77.6 1.9 %copy.11 = f32[16,16,512]{2,1,0:T(8,128)} copy(f32[16,16,512]{2,1,0:T(8,128)} %bitcast.7) | data formatting | bytes 1048576
  79.6 0.0 copy-done
  79.6 0.8 copy.12
Async XLA Ops:
  77.6 2.0 %copy-start = (f32[256,512]{1,0:T(8,128)S(1)}, f32[256,512]{1,0:T(8,128)}, u32[]{:S(2)}) copy-start(f32[256,512]{1,0:T(8,128)} %get-tuple-element.5) | copy-start | bytes 1572868

commit v3 on v2

--- a/solution.py
+++ b/solution.py
@@ -60,27 +60,28 @@
     rhs_v, x_in, dp_v, di_v, dr_v, bd_v, sg_v,
     cx, ce, xx, p0, p1, p2, p3, basis,
     x_out, x_side, f_out, f_side, h_out, h_side,
-    rs_out, rs_buf, as_buf, ac_buf, ag_buf, packed_v,
+    rs_out, rs_buf, as_buf, ag_buf, packed_v,
     in_sem, c_send, c_recv, x_send, x_recv, h_send, h_recv,
     sum_send, sum_recv,
 ):
     px, qy = lax.axis_index("px"), lax.axis_index("qy")
     y, x = px // CHIPS_X, px % CHIPS_X
     z, core = qy // CORES, qy % CORES
-    ny, nz, nxc = npx // CHIPS_X, nqy // CORES, CHIPS_X * CORES
-    xc = x * CORES + core
-
-    def along_z(s):
-        there = lax.rem(z + s, nz)
-        return there, {"px": px, "qy": there * CORES + core}
-
-    def along_y(s):
-        there = lax.rem(y + s, ny)
-        return there, {"px": there * CHIPS_X + x, "qy": qy}
-
-    def along_xc(s):
-        there = lax.rem(xc + s, nxc)
-        return there, {"px": y * CHIPS_X + there // CORES, "qy": z * CORES + there % CORES}
+    ny, nz = npx // CHIPS_X, nqy // CORES
+    nquad = nz // 2
+    nnear, nfar = CHIPS_X * CORES * 2, ny * nquad
+    near = (x * CORES + core) * 2 + z % 2
+    far = y * nquad + z // 2
+
+    def along_near(s):
+        there = lax.rem(near + s, nnear)
+        at_x, at_core, at_z = there // (2 * CORES), there // 2 % CORES, z - z % 2 + there % 2
+        return there, {"px": y * CHIPS_X + at_x, "qy": at_z * CORES + at_core}
+
+    def along_far(s):
+        there = lax.rem(far + s, nfar)
+        at_y, at_z = there // nquad, there % nquad * 2 + z % 2
+        return there, {"px": at_y * CHIPS_X + x, "qy": at_z * CORES + core}
 
     loads = []
     pairs = [(x_hbm.at[:, pl.ds(c * 128, 128)], x_in.at[c]) for c in range(TILES)]
@@ -108,7 +109,7 @@
         return {"px": px + a, "qy": qy + b}
 
     barrier = pltpu.get_barrier_semaphore()
-    count = jnp.int32(nz + ny + nxc - 3)
+    count = jnp.int32(nnear + nfar - 2)
     for a, b in AROUND:
         count += inside(a, b).astype(jnp.int32)
 
@@ -116,7 +117,7 @@
         def _():
             pl.semaphore_signal(barrier, inc=1, device_id=device(a, b), device_id_type=MESH)
 
-    for along, size in ((along_z, nz), (along_y, ny), (along_xc, nxc)):
+    for along, size in ((along_near, nnear), (along_far, nfar)):
         @pl.loop(1, size)
         def _(s):
             pl.semaphore_signal(barrier, inc=1, device_id=along(s)[1], device_id_type=MESH)
@@ -169,8 +170,7 @@
                 x_in[c, pl.ds(i, NR, stride=ROWS), :].reshape(2, 8, 128)
             )
 
-    @pl.loop(0, ROWS, unroll=4)
-    def _(i):
+    for i in range(ROWS):
         turn(i)
 
     def pack_rows(ref, first, out):
@@ -277,22 +277,19 @@
 
     def outer_rows_first(body, t):
         for begin in (0, ROWS - HALO):
-            @pl.loop(begin, begin + HALO, unroll=4)
-            def _(i):
+            for i in range(begin, begin + HALO):
                 body(i)
         if t < CYCLES:
             start(rim_rows(t))
-
-        @pl.loop(HALO, ROWS - HALO, unroll=4)
-        def _(i):
+        for i in range(HALO, ROWS - HALO):
             body(i)
 
     outer_rows_first(first_residual, 0)
 
     def total(t, local):
-        for j in range(nxc):
-            rs_out[j] = local[4 * j : 4 * j + 4]
-        rs_buf[t, xc] = rs_out[xc]
+        for j in range(nnear):
+            rs_out[j] = local[2 * j : 2 * j + 2]
+        rs_buf[t, near] = rs_out[near]
 
         def phase(n, along, size, src, buf, me):
             steps = [s for d in range(size // 2, 0, -1) for s in sorted({d, size - d})]
@@ -311,15 +308,13 @@
             whole.wait_recv()
             return whole
 
-        sent = [phase(0, along_xc, nxc, lambda there: rs_out.at[there], rs_buf, xc)]
-        as_buf[t, y] = jnp.sum(rs_buf[t], axis=0)
-        sent.append(phase(1, along_y, ny, lambda there: as_buf.at[t, y], as_buf, y))
-        ac_buf[t, z] = jnp.sum(as_buf[t], axis=0)
-        sent.append(phase(2, along_z, nz, lambda there: ac_buf.at[t, z], ac_buf, z))
-        ag_buf[t, xc] = jnp.sum(ac_buf[t], axis=0)
-        sent.append(phase(3, along_xc, nxc, lambda there: ag_buf.at[t, xc], ag_buf, xc))
-        for j in range(nxc):
-            packed_v[pl.ds(4 * j, 4), :] = ag_buf[t, j]
+        sent = [phase(0, along_near, nnear, lambda there: rs_out.at[there], rs_buf, near)]
+        as_buf[t, far] = jnp.sum(rs_buf[t], axis=0)
+        sent.append(phase(1, along_far, nfar, lambda there: as_buf.at[t, far], as_buf, far))
+        ag_buf[t, near] = jnp.sum(as_buf[t], axis=0)
+        sent.append(phase(2, along_near, nnear, lambda there: ag_buf.at[t, near], ag_buf, near))
+        for j in range(nnear):
+            packed_v[pl.ds(2 * j, 2), :] = ag_buf[t, j]
         return packed_v[...], sent
 
     def solve(both):
@@ -362,8 +357,7 @@
         start(beside)
         start(corner)
 
-        @pl.loop(0, ROWS, unroll=4)
-        def _(i):
+        for i in range(ROWS):
             keep_limbs(i, STEPS, p0[t, HALO + i])
 
         if t == 0:
@@ -389,16 +383,14 @@
                 p0[t, p, h, :, pl.ds(COLS, 128)] = unpack(tile, 2 * (row % 8) + h)
 
         def advance(k, rows, inner):
-            images = [
-                image_row(
-                    fields[k][p - 1], fields[k][p], fields[k][p + 1], p,
+            for p, own_row in zip(rows, inner):
+                center = fields[k][p]
+                image = image_row(
+                    fields[k][p - 1], center, fields[k][p + 1], p,
                     WIDE if k < STEPS - 1 else COLS,
                 )
-                for p in rows
-            ]
-            for p, image, own_row in zip(rows, images, inner):
                 if k < STEPS - 1:
-                    fields[k + 1][p] = image * (1.0 / THETA) - fields[k][p] * (SIGMA / THETA)
+                    fields[k + 1][p] = image * (1.0 / THETA) - center * (SIGMA / THETA)
                 if own_row:
                     keep_limbs(p - HALO, k, image)
 
@@ -406,10 +398,8 @@
         for p in range(HALO, HALO + ROWS):
             lanes_around(p)
         for k in range(STEPS):
-            @pl.loop(0, (EXT - 10 - 2 * k) // 2)
-            def _(i):
-                p = HALO + 1 + k + 2 * i
-                advance(k, [p, p + 1], [True, True])
+            rows = range(HALO + 1 + k, HALO + ROWS - 1 - k)
+            advance(k, rows, [True] * len(rows))
 
         def gram_step(i, acc):
             for n in range(4):
@@ -419,7 +409,7 @@
                 )
             return acc
 
-        acc = lax.fori_loop(1, 3, gram_step, jnp.zeros((3 * BASIS, 3 * BASIS), F32))
+        acc = gram_step(2, gram_step(1, jnp.zeros((3 * BASIS, 3 * BASIS), F32)))
 
         arrive(rims)
         arrive(corner)
@@ -430,11 +420,7 @@
             for begin in (k + 1, EXT - 5 - k):
                 rows = [begin + n for n in range(4)]
                 inner = [HALO <= p < HALO + ROWS for p in rows]
-                if k == STEPS - 1:
-                    advance(k, rows, inner)
-                else:
-                    advance(k, rows[:2], inner[:2])
-                    advance(k, rows[2:], inner[2:])
+                advance(k, rows, inner)
 
         acc = gram_step(3, gram_step(0, acc))
         rows = acc[2 * BASIS :] + acc[BASIS : 2 * BASIS] + acc[:BASIS]
@@ -473,17 +459,12 @@
         blocks.append(jnp.zeros((48, 128), F32))
         weights = jnp.concatenate(blocks, axis=0).T[64:96, :BASIS]
         high, mid, low = limbs(weights)
-        two = jnp.concatenate([high, mid], axis=0)
         three = jnp.concatenate([high, mid, low], axis=0)
+        three = jnp.concatenate([three] * 3, axis=1)
 
         def update(i):
-            def product(w, n):
-                return jnp.dot(
-                    w, basis[i, pl.ds(n * BASIS, BASIS), :], preferred_element_type=F32
-                )
-
-            d, f, g = product(three, 0), product(two, 1), product(high, 2)
-            change = ((d[64:] + f[32:] + g) + (d[32:64] + f[:32])) + d[:32]
+            parts = jnp.dot(three, basis[i], preferred_element_type=F32)
+            change = (parts[64:] + parts[32:64]) + parts[:32]
             res = p0[t, HALO + i, :, :, pl.ds(0, COLS)] + change[:NR].reshape(2, 8, COLS)
             sol = xx[1 + i, :, :, pl.ds(0, COLS)] + change[NR:].reshape(2, 8, COLS)
             if last:
@@ -520,7 +501,7 @@
         plane = vmem((ROWS, COLS), F32)
         marks = vmem((ROWS, COLS), jnp.int32)
         turned = vmem((TILES, NR * ROWS, 128), F32)
-        eighth = vmem((CYCLES, 8, 4, 128), F32)
+        sixteenth = vmem((CYCLES, 16, 2, 128), F32)
         sol, res = pl.pallas_call(
             lambda *refs: kernel(npx, nqy, *refs),
             out_shape=(flat, flat),
@@ -537,12 +518,12 @@
                 vmem((2, 8, 128), F32), vmem((2, 4, 8, 128), F32),
                 vmem((2, 8, 128), F32), vmem((2, 4, 8, 128), F32),
                 vmem((CYCLES, 2, 8, 128), F32), vmem((CYCLES, 2, 4, 8, 128), F32),
-                vmem((8, 4, 128), F32), eighth, eighth, eighth, eighth,
+                vmem((16, 2, 128), F32), sixteenth, vmem((CYCLES, 32, 2, 128), F32), sixteenth,
                 vmem((32, 128), F32),
                 dma((5 + 2 * TILES,)),
                 dma((8,)), dma((8,)), dma((8,)), dma((8,)),
                 dma((CYCLES, 8)), dma((CYCLES, 8)),
-                dma((4,)), dma((CYCLES, 4)),
+                dma((3,)), dma((CYCLES, 3)),
             ],
             compiler_params=pltpu.CompilerParams(
                 collective_id=0, has_side_effects=True, vmem_limit_bytes=62 * 1024 * 1024

time: 80.5 us -> 77 us (0.957)
  Pallas kernels: 77 us -> 73.5 us
    pallas_call x1, Pallas kernels: 77 us -> 73.5 us  [per_device(): pl.pallas_call(lambda *refs: kernel(npx, nqy, *refs), out_shape=(flat, fl...]
where the time goes in v3:
time: 77 us; the launch traced here: 76.9 us
  Pallas kernels  73.5 us (95%)
  local copies, waits for them, and re-layouts  2.74 us (4%)
    pallas_call x1, Pallas kernels, per_device(): pl.pallas_call(lambda *refs: kernel(npx, nqy, *refs), out_shape=(flat, fl...  73.5 us
    unnamed x4, local copies, waits for them, and re-layouts  2.74 us

profile of v3, /device:TPU:1, one launch (start us, length us, event | category | flops | bytes accessed | tf_op | source)
XLA Modules:
  0.0 76.9 jit_solution(12900836272673310866)
XLA Ops:
  0.6 73.5 %shard_map.86 = (f32[256,512]{1,0:T(8,128)}, f32[256,512]{1,0:T(8,128)}) custom-call(f32[256,512]{1,0:T(8,128)} %bitcast.4, f32[256,512]{1,0:T(8,128)} %bitcast.5, f32[16,512]{1,0:T(8,128)} %refs_2_.1, f32[16,512]{1,0:T(8,128)} %refs_3_.1, f32[16,512]{1,0:T(8,128)} %refs_4_.1, s32[16,512]{1,0:T(8,128)} %refs_5_.1, s32[16,512]{1,0:T(8,128)} %refs_6_.1), custom_call_target="tpu_custom_call" | custom-call | tf_op jit(solution)/shard_map/pallas_call | solution.py:505
  74.1 0.0 copy-start
  74.1 1.9 %copy.11 = f32[16,16,512]{2,1,0:T(8,128)} copy(f32[16,16,512]{2,1,0:T(8,128)} %bitcast.7) | data formatting | bytes 1048576
  76.1 0.0 copy-done
  76.1 0.8 %copy.12 = f32[16,16,512]{2,1,0:T(8,128)} copy(f32[16,16,512]{2,1,0:T(8,128)S(1)} %bitcast.6) | data formatting | bytes 1048576
Async XLA Ops:
  74.1 2.0 %copy-start = (f32[256,512]{1,0:T(8,128)S(1)}, f32[256,512]{1,0:T(8,128)}, u32[]{:S(2)}) copy-start(f32[256,512]{1,0:T(8,128)} %get-tuple-element.5) | copy-start | bytes 1572868

commit v4 on v3

--- a/solution.py
+++ b/solution.py
@@ -56,9 +56,9 @@
 def kernel(
     npx, nqy,
     rhs_hbm, x_hbm, dp_hbm, di_hbm, dr_hbm, bd_hbm, sg_hbm,
-    sol_hbm, res_hbm,
+    basis, sol_out, res_out, weights_out,
     rhs_v, x_in, dp_v, di_v, dr_v, bd_v, sg_v,
-    cx, ce, xx, p0, p1, p2, p3, basis,
+    cx, ce, xx, p0, p1, p2, p3,
     x_out, x_side, f_out, f_side, h_out, h_side,
     rs_out, rs_buf, as_buf, ag_buf, packed_v,
     in_sem, c_send, c_recv, x_send, x_recv, h_send, h_recv,
@@ -83,6 +83,21 @@
         at_y, at_z = there // nquad, there % nquad * 2 + z % 2
         return there, {"px": at_y * CHIPS_X + x, "qy": at_z * CORES + core}
 
+    def inside(a, b):
+        return (px + a >= 0) & (px + a < npx) & (qy + b >= 0) & (qy + b < nqy)
+
+    def device(a, b):
+        return {"px": px + a, "qy": qy + b}
+
+    barrier = pltpu.get_barrier_semaphore()
+    count = jnp.int32(nnear + nfar - 2)
+    for a, b in AROUND:
+        count += inside(a, b).astype(jnp.int32)
+
+        @pl.when(inside(a, b))
+        def _():
+            pl.semaphore_signal(barrier, inc=1, device_id=device(a, b), device_id_type=MESH)
+
     loads = []
     pairs = [(x_hbm.at[:, pl.ds(c * 128, 128)], x_in.at[c]) for c in range(TILES)]
     pairs += [(dp_hbm, dp_v), (di_hbm, di_v), (dr_hbm, dr_v), (bd_hbm, bd_v), (sg_hbm, sg_v)]
@@ -92,35 +107,33 @@
         load.start()
         loads.append(load)
 
-    for edge in (0, 24):
-        cx[:, pl.ds(edge, 8), :] = jnp.zeros((3, 8, COLS), F32)
-    for edge in (0, ROWS + 1):
-        xx[edge] = jnp.zeros((2, 8, WIDE), F32)
-    for side in (x_side, f_side, h_side):
-        side[...] = jnp.zeros_like(side)
-    for t in range(CYCLES):
-        for edge in (0, HALO + ROWS):
-            p0[t, pl.ds(edge, HALO), :, :, pl.ds(0, COLS)] = jnp.zeros((HALO, 2, 8, COLS), F32)
-
-    def inside(a, b):
-        return (px + a >= 0) & (px + a < npx) & (qy + b >= 0) & (qy + b < nqy)
-
-    def device(a, b):
-        return {"px": px + a, "qy": qy + b}
-
-    barrier = pltpu.get_barrier_semaphore()
-    count = jnp.int32(nnear + nfar - 2)
-    for a, b in AROUND:
-        count += inside(a, b).astype(jnp.int32)
-
-        @pl.when(inside(a, b))
-        def _():
-            pl.semaphore_signal(barrier, inc=1, device_id=device(a, b), device_id_type=MESH)
-
     for along, size in ((along_near, nnear), (along_far, nfar)):
         @pl.loop(1, size)
         def _(s):
             pl.semaphore_signal(barrier, inc=1, device_id=along(s)[1], device_id_type=MESH)
+
+    for a, b in AROUND:
+        @pl.when(jnp.logical_not(inside(a, b)))
+        def _():
+            if b == 0:
+                edge = 0 if a < 0 else 24
+                cx[:, pl.ds(edge, 8), :] = jnp.zeros((3, 8, COLS), F32)
+                edge = 0 if a < 0 else ROWS + 1
+                xx[edge, :, :, pl.ds(0, COLS)] = jnp.zeros((2, 8, COLS), F32)
+                edge = 0 if a < 0 else HALO + ROWS
+                for t in range(CYCLES):
+                    p0[t, pl.ds(edge, HALO), :, :, pl.ds(0, COLS)] = (
+                        jnp.zeros((HALO, 2, 8, COLS), F32)
+                    )
+                return
+            s = 0 if b < 0 else 1
+            tiles = {-1: (0,), 0: (1, 2), 1: (3,)}[a]
+            for n in tiles:
+                if a == 0:
+                    x_side[s, n] = jnp.zeros((8, 128), F32)
+                f_side[s, n] = jnp.zeros((8, 128), F32)
+                for t in range(CYCLES):
+                    h_side[t, s, n] = jnp.zeros((8, 128), F32)
 
     def start(copies):
         for (a, b), copy in copies:
@@ -462,27 +475,39 @@
         three = jnp.concatenate([high, mid, low], axis=0)
         three = jnp.concatenate([three] * 3, axis=1)
 
+        if last:
+            weights_out[...] = three
+            break
+
         def update(i):
-            parts = jnp.dot(three, basis[i], preferred_element_type=F32)
-            change = (parts[64:] + parts[32:64]) + parts[:32]
-            res = p0[t, HALO + i, :, :, pl.ds(0, COLS)] + change[:NR].reshape(2, 8, COLS)
-            sol = xx[1 + i, :, :, pl.ds(0, COLS)] + change[NR:].reshape(2, 8, COLS)
-            if last:
-                for c in range(TILES):
-                    part = slice(c * 128, c * 128 + 128)
-                    rhs_v[c, pl.ds(i, NR, stride=ROWS), :] = res[:, :, part].reshape(NR, 128)
-                    x_in[c, pl.ds(i, NR, stride=ROWS), :] = sol[:, :, part].reshape(NR, 128)
-            else:
-                p0[t + 1, HALO + i, :, :, pl.ds(0, COLS)] = res
-                xx[1 + i, :, :, pl.ds(0, COLS)] = sol
+            change = combined(three, basis[i])
+            res = p0[t, HALO + i, :, :, pl.ds(0, COLS)] + change[0]
+            p0[t + 1, HALO + i, :, :, pl.ds(0, COLS)] = res
+            res_out[i] = res
+            sol_out[i] = xx[1 + i, :, :, pl.ds(0, COLS)] + change[1]
 
         outer_rows_first(update, t + 1)
 
+
+def combined(weights, rows):
+    parts = jnp.dot(weights, rows, preferred_element_type=F32)
+    change = (parts[64:] + parts[32:64]) + parts[:32]
+    return change[:NR].reshape(2, 8, COLS), change[NR:].reshape(2, 8, COLS)
+
+
+def finish(basis, sol_in, res_in, weights, sol_hbm, res_hbm, sol_v, res_v, sem):
+    for i in range(ROWS):
+        change = combined(weights[...], basis[i])
+        res, sol = res_in[i] + change[0], sol_in[i] + change[1]
+        for c in range(TILES):
+            part = slice(c * 128, c * 128 + 128)
+            res_v[c, pl.ds(i, NR, stride=ROWS), :] = res[:, :, part].reshape(NR, 128)
+            sol_v[c, pl.ds(i, NR, stride=ROWS), :] = sol[:, :, part].reshape(NR, 128)
     stores = []
-    for src, dst in ((x_in, sol_hbm), (rhs_v, res_hbm)):
+    for src, dst in ((sol_v, sol_hbm), (res_v, res_hbm)):
         for c in range(TILES):
             store = pltpu.make_async_copy(
-                src.at[c], dst.at[:, pl.ds(c * 128, 128)], in_sem.at[len(stores)]
+                src.at[c], dst.at[:, pl.ds(c * 128, 128)], sem.at[len(stores)]
             )
             store.start()
             stores.append(store)
@@ -502,11 +527,15 @@
         marks = vmem((ROWS, COLS), jnp.int32)
         turned = vmem((TILES, NR * ROWS, 128), F32)
         sixteenth = vmem((CYCLES, 16, 2, 128), F32)
-        sol, res = pl.pallas_call(
+        held = jax.ShapeDtypeStruct((ROWS, 2, 8, COLS), F32)
+        parts = pl.pallas_call(
             lambda *refs: kernel(npx, nqy, *refs),
-            out_shape=(flat, flat),
+            out_shape=(
+                jax.ShapeDtypeStruct((ROWS, 3 * BASIS, COLS), BF16), held, held,
+                jax.ShapeDtypeStruct((96, 3 * BASIS), BF16),
+            ),
             in_specs=[pl.BlockSpec(memory_space=pl.ANY)] * 7,
-            out_specs=(pl.BlockSpec(memory_space=pl.ANY),) * 2,
+            out_specs=(pl.BlockSpec(memory_space=vmem),) * 4,
             scratch_shapes=[
                 turned, turned, plane, plane, plane, marks, marks,
                 vmem((3, ROWS + 16, COLS), F32),
@@ -514,7 +543,6 @@
                 vmem((ROWS + 2, 2, 8, WIDE), F32),
                 vmem((CYCLES, EXT, 2, 8, WIDE), F32),
                 field, field, field,
-                vmem((ROWS, 3 * BASIS, COLS), BF16),
                 vmem((2, 8, 128), F32), vmem((2, 4, 8, 128), F32),
                 vmem((2, 8, 128), F32), vmem((2, 4, 8, 128), F32),
                 vmem((CYCLES, 2, 8, 128), F32), vmem((CYCLES, 2, 4, 8, 128), F32),
@@ -526,9 +554,20 @@
                 dma((3,)), dma((CYCLES, 3)),
             ],
             compiler_params=pltpu.CompilerParams(
-                collective_id=0, has_side_effects=True, vmem_limit_bytes=62 * 1024 * 1024
+                collective_id=0, has_side_effects=True, vmem_limit_bytes=48 * 1024 * 1024
             ),
-        )(rhs.reshape(NR * ROWS, COLS), iterate.reshape(NR * ROWS, COLS), *fields)
+        )(*[
+            pltpu.with_memory_space_constraint(a, pltpu.HBM) for a in
+            (rhs.reshape(NR * ROWS, COLS), iterate.reshape(NR * ROWS, COLS)) + fields
+        ])
+        sol, res = pl.pallas_call(
+            finish,
+            out_shape=(flat, flat),
+            in_specs=[pl.BlockSpec(memory_space=vmem)] * 4,
+            out_specs=(pl.BlockSpec(memory_space=pl.ANY),) * 2,
+            scratch_shapes=[turned, turned, dma((2 * TILES,))],
+            compiler_params=pltpu.CompilerParams(vmem_limit_bytes=48 * 1024 * 1024),
+        )(*parts)
         return sol.reshape(NR, ROWS, COLS), res.reshape(NR, ROWS, COLS)
 
     whole, plane = P(None, "px", "qy"), P("px", "qy")

time: 77 us -> 73.9 us (0.960)
  local copies, waits for them, and re-layouts: 2.74 us -> 0 us
    unnamed x4 -> x0, local copies, waits for them, and re-layouts: 2.74 us -> none
    pallas_call x1 -> x2, Pallas kernels: 73.5 us -> 73.2 us  [the longest x1 71.2 us: per_device(): pl.pallas_call(lambda *refs: kernel(npx, nqy, *refs), out_shape=(jax.Shap...]
where the time goes in v4:
time: 73.9 us; the launch traced here: 73.8 us
  Pallas kernels  73.2 us (99%)
    pallas_call x1, Pallas kernels, per_device(): pl.pallas_call(lambda *refs: kernel(npx, nqy, *refs), out_shape=(jax.Shap...  71.2 us
    pallas_call x1, Pallas kernels, per_device(): pl.pallas_call(finish, out_shape=(flat, flat), in_specs=[pl.BlockSpec(mem...  1.96 us

profile of v4, /device:TPU:1, one launch (start us, length us, event | category | flops | bytes accessed | tf_op | source)
XLA Modules:
  0.0 73.8 jit_solution(14472475181118152745)
XLA Ops:
  0.6 71.2 %shard_map.86 = (bf16[16,240,512]{2,1,0:T(8,128)(2,1)S(1)}, f32[16,2,8,512]{3,2,1,0:T(8,128)S(1)}, f32[16,2,8,512]{3,2,1,0:T(8,128)S(1)}, bf16[96,240]{1,0:T(8,128)(2,1)S(1)}) custom-call(f32[256,512]{1,0:T(8,128)} %bitcast.4, f32[256,512]{1,0:T(8,128)} %bitcast.5, f32[16,512]{1,0:T(8,128)} %refs_2_.1, f32[16,512]{1,0:T(8,128)} %refs_3_.1, ...), custom_call_target="tpu_custom_call" | custom-call | tf_op jit(solution)/shard_map/pallas_call | solution.py:531
  71.8 2.0 %shard_map.87 = (f32[256,512]{1,0:T(8,128)}, f32[256,512]{1,0:T(8,128)}) custom-call(bf16[16,240,512]{2,1,0:T(8,128)(2,1)S(1)} %get-tuple-element.8.basis, f32[16,2,8,512]{3,2,1,0:T(8,128)S(1)} %get-tuple-element.9.sol_in, f32[16,2,8,512]{3,2,1,0:T(8,128)S(1)} %get-tuple-element.10.res_in, bf16[96,240]{1,0:T(8,128)(2,1)S(1)} %get-tuple-element.11.weights), custom_call_target="tpu_custom_call" | custom-call | tf_op jit(solution)/shard_map/pallas_call | solution.py:563

commit v5 on v4

--- a/solution.py
+++ b/solution.py
@@ -10,6 +10,7 @@
 SIGMA = 5.5
 THETA = 4.5
 HALO = STEPS
+PIECES = 4
 NR = 16
 ROWS = 16
 COLS = 512
@@ -61,7 +62,7 @@
     cx, ce, xx, p0, p1, p2, p3,
     x_out, x_side, f_out, f_side, h_out, h_side,
     rs_out, rs_buf, as_buf, ag_buf, packed_v,
-    in_sem, c_send, c_recv, x_send, x_recv, h_send, h_recv,
+    in_sem, c_send, c_recv, x_send, x_recv, h_send, h_recv, r_send, r_recv,
     sum_send, sum_recv,
 ):
     px, qy = lax.axis_index("px"), lax.axis_index("qy")
@@ -267,7 +268,6 @@
         tile = both_sides(x_side, 1 + i // 8)
         for h in range(2):
             xx[1 + i, h, :, pl.ds(COLS, 128)] = unpack(tile, 2 * (i % 8) + h)
-    arrive(x_rows)
 
     def first_residual(i):
         value = image_row(xx[i], xx[1 + i], xx[2 + i], HALO + i, COLS)
@@ -280,24 +280,31 @@
     def rim_rows(t):
         copies = []
         for a in (-1, 1):
-            n = AROUND.index((a, 0))
-            copies.append(remote(
-                p0.at[t, pl.ds(HALO if a < 0 else ROWS, HALO), :, :, pl.ds(0, COLS)],
-                p0.at[t, pl.ds(HALO + ROWS if a < 0 else 0, HALO), :, :, pl.ds(0, COLS)],
-                h_send.at[t, n], h_recv.at[t, n], a, 0,
-            ))
+            for n in range(PIECES):
+                begin = n * HALO // PIECES
+                size = HALO // PIECES
+                src = (HALO if a < 0 else ROWS) + begin
+                dst = (HALO + ROWS if a < 0 else 0) + begin
+                copies.append(remote(
+                    p0.at[t, pl.ds(src, size), :, :, pl.ds(0, COLS)],
+                    p0.at[t, pl.ds(dst, size), :, :, pl.ds(0, COLS)],
+                    r_send.at[t, (a + 1) // 2, n], r_recv.at[t, (a + 1) // 2, n], a, 0,
+                ))
         return copies
 
-    def outer_rows_first(body, t):
-        for begin in (0, ROWS - HALO):
-            for i in range(begin, begin + HALO):
-                body(i)
+    def outer_rows_first(body, t, before_ends=None):
+        for i in (1, 2, 3, 12, 13, 14):
+            body(i)
+        if before_ends is not None:
+            before_ends()
+        for i in (0, 15):
+            body(i)
         if t < CYCLES:
             start(rim_rows(t))
         for i in range(HALO, ROWS - HALO):
             body(i)
 
-    outer_rows_first(first_residual, 0)
+    outer_rows_first(first_residual, 0, lambda: arrive(x_rows))
 
     def total(t, local):
         for j in range(nnear):
@@ -492,25 +499,29 @@
 def combined(weights, rows):
     parts = jnp.dot(weights, rows, preferred_element_type=F32)
     change = (parts[64:] + parts[32:64]) + parts[:32]
-    return change[:NR].reshape(2, 8, COLS), change[NR:].reshape(2, 8, COLS)
+    width = rows.shape[-1]
+    return change[:NR].reshape(2, 8, width), change[NR:].reshape(2, 8, width)
 
 
 def finish(basis, sol_in, res_in, weights, sol_hbm, res_hbm, sol_v, res_v, sem):
-    for i in range(ROWS):
-        change = combined(weights[...], basis[i])
-        res, sol = res_in[i] + change[0], sol_in[i] + change[1]
-        for c in range(TILES):
-            part = slice(c * 128, c * 128 + 128)
-            res_v[c, pl.ds(i, NR, stride=ROWS), :] = res[:, :, part].reshape(NR, 128)
-            sol_v[c, pl.ds(i, NR, stride=ROWS), :] = sol[:, :, part].reshape(NR, 128)
     stores = []
-    for src, dst in ((sol_v, sol_hbm), (res_v, res_hbm)):
-        for c in range(TILES):
-            store = pltpu.make_async_copy(
-                src.at[c], dst.at[:, pl.ds(c * 128, 128)], sem.at[len(stores)]
-            )
-            store.start()
-            stores.append(store)
+    for begin in range(0, COLS, 256):
+        cols = slice(begin, begin + 256)
+        for i in range(ROWS):
+            change = combined(weights[...], basis[i, :, cols])
+            res, sol = res_in[i, :, :, cols] + change[0], sol_in[i, :, :, cols] + change[1]
+            for c in range(2):
+                part = slice(c * 128, c * 128 + 128)
+                tile = begin // 128 + c
+                res_v[tile, pl.ds(i, NR, stride=ROWS), :] = res[:, :, part].reshape(NR, 128)
+                sol_v[tile, pl.ds(i, NR, stride=ROWS), :] = sol[:, :, part].reshape(NR, 128)
+        for src, dst in ((sol_v, sol_hbm), (res_v, res_hbm)):
+            for tile in (begin // 128, begin // 128 + 1):
+                store = pltpu.make_async_copy(
+                    src.at[tile], dst.at[:, pl.ds(tile * 128, 128)], sem.at[len(stores)]
+                )
+                store.start()
+                stores.append(store)
     for store in stores:
         store.wait()
 
@@ -551,6 +562,7 @@
                 dma((5 + 2 * TILES,)),
                 dma((8,)), dma((8,)), dma((8,)), dma((8,)),
                 dma((CYCLES, 8)), dma((CYCLES, 8)),
+                dma((CYCLES, 2, PIECES)), dma((CYCLES, 2, PIECES)),
                 dma((3,)), dma((CYCLES, 3)),
             ],
             compiler_params=pltpu.CompilerParams(

time: 73.9 us -> 73.9 us (level)
  no operation moved by 1% of the time
where the time goes in v5:
time: 73.9 us; the launch traced here: 73.8 us
  Pallas kernels  73.1 us (99%)
    pallas_call x1, Pallas kernels, per_device(): pl.pallas_call(lambda *refs: kernel(npx, nqy, *refs), out_shape=(jax.Shap...  71.4 us
    pallas_call x1, Pallas kernels, per_device(): pl.pallas_call(finish, out_shape=(flat, flat), in_specs=[pl.BlockSpec(mem...  1.71 us

profile of v5, /device:TPU:1, one launch (start us, length us, event | category | flops | bytes accessed | tf_op | source)
XLA Modules:
  0.0 73.8 jit_solution(922697581153903168)
XLA Ops:
  0.6 71.4 %shard_map.86 = (bf16[16,240,512]{2,1,0:T(8,128)(2,1)S(1)}, f32[16,2,8,512]{3,2,1,0:T(8,128)S(1)}, f32[16,2,8,512]{3,2,1,0:T(8,128)S(1)}, bf16[96,240]{1,0:T(8,128)(2,1)S(1)}) custom-call(f32[256,512]{1,0:T(8,128)} %bitcast.4, f32[256,512]{1,0:T(8,128)} %bitcast.5, f32[16,512]{1,0:T(8,128)} %refs_2_.1, f32[16,512]{1,0:T(8,128)} %refs_3_.1, ...), custom_call_target="tpu_custom_call" | custom-call | tf_op jit(solution)/shard_map/pallas_call | solution.py:542
  72.1 1.7 %shard_map.87 = (f32[256,512]{1,0:T(8,128)}, f32[256,512]{1,0:T(8,128)}) custom-call(bf16[16,240,512]{2,1,0:T(8,128)(2,1)S(1)} %get-tuple-element.8.basis, f32[16,2,8,512]{3,2,1,0:T(8,128)S(1)} %get-tuple-element.9.sol_in, f32[16,2,8,512]{3,2,1,0:T(8,128)S(1)} %get-tuple-element.10.res_in, bf16[96,240]{1,0:T(8,128)(2,1)S(1)} %get-tuple-element.11.weights), custom_call_target="tpu_custom_call" | custom-call | tf_op jit(solution)/shard_map/pallas_call | solution.py:575
